TPU v7x, 32 devices: a whole 2x2x4 slice. The times are simulated.
32 devices in a mesh: row: 4 (over z), col: 2 (over x), rep: 4 (over y, core).
Axes of the slice: x: 2, y: 2, z: 4, core: 2. Of those that a mesh axis runs over, the one named last changes fastest.
Arguments:
- features: bfloat16 [8192, 256], P(('col', 'rep'), 'row'), may hold values from -6 to 6
- weight: bfloat16 [256, 256], replicated, may hold values from -0.375 to 0.375
- cotangent: bfloat16 [8192, 256], P(('row', 'col', 'rep')), may hold values from -6 to 6
- block_values: bfloat16 [4, 8, 128, 128, 128], P('row', ('col', 'rep')), may hold values from -0.0625 to 0.0625
- block_coords: int32 [4, 8, 128, 2], P('row', ('col', 'rep')), may hold values from 0 to 15, as said below
- block_counts: int32 [4, 8], P('row', ('col', 'rep')), may hold values from 1 to 128, as said below
Outputs:
- activations: bfloat16 [8192, 256], P(('row', 'col', 'rep'))
- input_grad: bfloat16 [8192, 256], P(('col', 'rep'), 'row')
- weight_grad: float32 [256, 256], replicated
Inputs may be any that keep to these rules, and one draw needn't show every extreme that they name: `block_coords`: each slot's row block is below 16 and its column block below 8. `block_counts`: some tile uses all 128 slots.
All inputs are finite; a program needn't handle non-finite values.
Results may differ from a plain program's by a relative error of at most 0.014.
Values may be sent and summed in bfloat16 or wider, within the bound.
A program may use at most 128 MiB of HBM per device.

v0:
```python
import math
import jax
import jax.numpy as jnp
from jax import lax
from jax.sharding import PartitionSpec as P


def local(features, weight, cotangent, block_values, block_coords, block_counts):
    blocks = block_values[0, 0]
    coords = block_coords[0, 0]
    live_count = block_counts[0, 0]
    slots = blocks.shape[0]
    gathered = lax.all_gather(features, "row", axis=1, tiled=True)
    feat_width = gathered.shape[1]
    col_blocks = gathered.shape[0] // 128
    row_blocks = cotangent.shape[0] * lax.axis_size(("col", "rep")) // 128
    feat_blocks = gathered.reshape(col_blocks, 128, feat_width)
    is_live = (jnp.arange(slots, dtype=jnp.int32) < live_count).astype(jnp.float32)
    per_turn = math.gcd(slots, 64)
    rounds = slots // per_turn
    pieces = (
        blocks.reshape(rounds, per_turn, 128, 128),
        coords[:, 0].reshape(rounds, per_turn),
        coords[:, 1].reshape(rounds, per_turn),
        is_live.reshape(rounds, per_turn),
    )

    def forward_step(total, piece):
        blocks_g, rows_g, cols_g, live_g = piece
        chosen = feat_blocks[cols_g]
        product = jnp.einsum("bij,bjf->bif", blocks_g, chosen, preferred_element_type=jnp.float32)
        return (total.at[rows_g].add(product * live_g[:, None, None]), None)

    partial_value, _ = lax.scan(
        forward_step, jnp.zeros((row_blocks, 128, feat_width), jnp.float32), pieces
    )
    partial_value = partial_value.reshape(row_blocks * 128, feat_width)
    summed = lax.psum_scatter(partial_value, ("col", "rep"), scatter_dimension=0, tiled=True)
    aggregate = summed.astype(jnp.bfloat16)
    pre_act = jnp.dot(aggregate, weight, preferred_element_type=jnp.float32)
    sigma = jax.nn.sigmoid(pre_act)
    activations = (pre_act * sigma).astype(jnp.bfloat16)
    grad_pre = (cotangent.astype(jnp.float32) * sigma * (1.0 + pre_act * (1.0 - sigma))).astype(
        jnp.bfloat16
    )
    weight_terms = jnp.dot(aggregate.T, grad_pre, preferred_element_type=jnp.float32)
    share = lax.psum_scatter(
        weight_terms.astype(jnp.bfloat16), ("col", "rep"), scatter_dimension=0, tiled=True
    ).astype(jnp.float32)
    share = lax.psum(share, "row")
    weight_grad = lax.all_gather(share, ("col", "rep"), axis=0, tiled=True)
    back_rows = jnp.dot(grad_pre, weight.T, preferred_element_type=jnp.float32).astype(jnp.bfloat16)
    back_all = lax.all_gather(back_rows, ("col", "rep"), axis=0, tiled=True)
    back_blocks = back_all.reshape(row_blocks, 128, back_all.shape[1])

    def backward_step(total, piece):
        blocks_g, rows_g, cols_g, live_g = piece
        chosen = back_blocks[rows_g]
        product = jnp.einsum("bji,bjf->bif", blocks_g, chosen, preferred_element_type=jnp.float32)
        return (total.at[cols_g].add(product * live_g[:, None, None]), None)

    grad_terms, _ = lax.scan(
        backward_step, jnp.zeros((col_blocks, 128, back_all.shape[1]), jnp.float32), pieces
    )
    grad_terms = grad_terms.reshape(col_blocks * 128, back_all.shape[1])
    input_grad = lax.psum_scatter(
        grad_terms.astype(jnp.bfloat16), "row", scatter_dimension=1, tiled=True
    )
    return (activations, input_grad, weight_grad)


def solution(mesh):
    in_specs = (
        P(("col", "rep"), "row"),
        P(),
        P(("row", "col", "rep"), None),
        P("row", ("col", "rep"), None, None, None),
        P("row", ("col", "rep"), None, None),
        P("row", ("col", "rep")),
    )
    out_specs = (P(("row", "col", "rep"), None), P(("col", "rep"), "row"), P())
    return jax.shard_map(local, mesh=mesh, in_specs=in_specs, out_specs=out_specs, check_vma=False)
```

profile of v0, /device:TPU:0, one launch (start us, length us, event | category | flops | bytes accessed | tf_op | source)
XLA Modules:
  0.0 228.0 jit_solution(13461801693741192329)
XLA Ops:
  8.8 17.6 %all_gather.9 = bf16[1024,256]{0,1:T(8,128)(2,1)S(1)} all-gather(bf16[1024,64]{0,1:T(8,128)(2,1)} %param.10), channel_id=1, replica_groups=mesh['row'=4,'col'=2,'rep'=4] {'row'}, dimensions={1}, use_global_device_ids=true | all-gather | bytes 655360 | tf_op jit(solution)/shard_map/all_gather | solution.py:13
  26.8 45.1 %while.20 = (s32[]{:T(128)}, f32[16,128,256]{2,1,0:T(8,128)S(1)}, s32[2,64]{1,0:T(2,128)S(1)}, bf16[2,64,128,128]{3,2,1,0:T(8,128)(2,1)}, s32[2,64]{1,0:T(2,128)...) while((s32[]{:T(128)}, f32[16,128,256]{2,1,0:T(8,128)S(1)}, ...), condition=%wide.region_2.3_spmd, body=%wide.region_0.2_spmd.sunk | while | flops 541066624 | bytes 48241756 | solution.py:34
  26.9 2.8 %gather_fusion = bf16[64,128,256]{2,1,0:T(8,128)(2,1)} fusion(bf16[8,128,256]{2,1,0:T(8,128)(2,1)S(1)} %get-tuple-element.237, s32[1024]{0:T(1024)S(1)} %pad_clamp_fusion.4), kind=kCustom, calls=%fused_computation.clone.1 | custom fusion | bytes 8388864 | tf_op jit(solution)/shard_map/while/body/eval_jaxpr/gather | solution.py:30
  29.7 7.3 %broadcast_multiply_fusion.4 = f32[64,128,256]{2,1,0:T(8,128)} fusion(f32[64]{0:T(128)S(1)} %fusion.36, bf16[64,128,256]{2,1,0:T(8,128)(2,1)} %gather_fusion, bf16[2,64,128,128]{3,2,1,0:T(8,128)(2,1)} %get-tuple-element.235, s32[]{:T(128)} %get-tuple-element.224), kind=kOutput, calls=%fused_computation.4.clone.1 | convolution fusion | flops 538968064 | bytes 14680832 | tf_op jit(solution)/shard_map/while/body/eval_jaxpr/bij,bjf->bif/dot_general | solution.py:31
  37.0 12.4 %scatter_fusion = f32[16,128,256]{2,1,0:T(8,128)S(1)} fusion(f32[16,128,256]{2,1,0:T(8,128)S(1)} %get-tuple-element.225, s32[64]{0:T(128)S(1)} %get-tuple-element.205, f32[64,128,256]{2,1,0:T(8,128)} %broadcast_multiply_fusion.4), kind=kCustom, calls=%fused_computation.2.clone.1 | custom fusion | flops 2097152 | bytes 25166080 | tf_op jit(solution)/shard_map/while/body/eval_jaxpr/scatter-add | solution.py:32
  49.4 2.8 %gather_fusion = bf16[64,128,256]{2,1,0:T(8,128)(2,1)} fusion(bf16[8,128,256]{2,1,0:T(8,128)(2,1)S(1)} %get-tuple-element.237, s32[1024]{0:T(1024)S(1)} %pad_clamp_fusion.4), kind=kCustom, calls=%fused_computation.clone.1 | custom fusion | bytes 8388864 | tf_op jit(solution)/shard_map/while/body/eval_jaxpr/gather | solution.py:30
  52.2 7.3 %broadcast_multiply_fusion.4 = f32[64,128,256]{2,1,0:T(8,128)} fusion(f32[64]{0:T(128)S(1)} %fusion.36, bf16[64,128,256]{2,1,0:T(8,128)(2,1)} %gather_fusion, bf16[2,64,128,128]{3,2,1,0:T(8,128)(2,1)} %get-tuple-element.235, s32[]{:T(128)} %get-tuple-element.224), kind=kOutput, calls=%fused_computation.4.clone.1 | convolution fusion | flops 538968064 | bytes 14680832 | tf_op jit(solution)/shard_map/while/body/eval_jaxpr/bij,bjf->bif/dot_general | solution.py:31
  59.5 12.4 %scatter_fusion = f32[16,128,256]{2,1,0:T(8,128)S(1)} fusion(f32[16,128,256]{2,1,0:T(8,128)S(1)} %get-tuple-element.225, s32[64]{0:T(128)S(1)} %get-tuple-element.205, f32[64,128,256]{2,1,0:T(8,128)} %broadcast_multiply_fusion.4), kind=kCustom, calls=%fused_computation.2.clone.1 | custom fusion | flops 2097152 | bytes 25166080 | tf_op jit(solution)/shard_map/while/body/eval_jaxpr/scatter-add | solution.py:32
  72.0 1.3 copy-done.1
  73.4 43.0 %reduce-scatter.4.cloned.1.call-done = f32[256,256]{1,0:T(8,128)} async-done(((f32[2048,256]{1,0:T(8,128)}), f32[256,256]{1,0:T(8,128)}) %reduce-scatter.4.cloned.1.call-update) | async-done | bytes 262160 | tf_op jit(solution)/shard_map/reduce_scatter | solution.py:38
  116.4 1.9 multiply_convert_fusion
  119.2 6.4 %copy.9 = bf16[1,1,128,128,128]{3,4,2,1,0:T(8,128)(2,1)} copy(bf16[1,1,128,128,128]{4,3,2,1,0:T(8,128)(2,1)} %bitcast.81) | data formatting | bytes 8388608 | tf_op args[3]
  125.6 0.9 convolution_convert_fusion
  126.6 16.1 %all-gather.2.cloned.1.call-done = bf16[2048,256]{1,0:T(8,128)(2,1)} async-done(((bf16[256,256]{1,0:T(8,128)(2,1)}), bf16[2048,256]{1,0:T(8,128)(2,1)}) %all-gather.2.cloned.1.call-update) | async-done | bytes 1048592 | tf_op jit(solution)/shard_map/all_gather | solution.py:53
  142.8 47.4 %while.21 = (s32[]{:T(128)}, f32[8,128,256]{2,1,0:T(8,128)S(1)}, s32[2,64]{1,0:T(2,128)S(1)}, bf16[2,64,128,128]{2,3,1,0:T(8,128)(2,1)}, s32[2,64]{1,0:T(2,128)S...) while((s32[]{:T(128)}, f32[8,128,256]{2,1,0:T(8,128)S(1)}, s32[2,64]{1,0:T(2,128)S(1)}, ...), condition=%wide.region_6.7_spmd, body=%wide.region_4.6_spmd.sunk | while | flops 541066624 | bytes 48241756 | solution.py:62
  142.8 4.0 %gather_fusion.1 = bf16[64,128,256]{2,1,0:T(8,128)(2,1)} fusion(bf16[16,128,256]{2,1,0:T(8,128)(2,1)} %get-tuple-element.261, s32[1024]{0:T(1024)S(1)} %pad_clamp_fusion.5), kind=kCustom, calls=%fused_computation.1.clone.1 | custom fusion | bytes 8388864 | tf_op jit(solution)/shard_map/while/body/eval_jaxpr/gather | solution.py:58
  146.8 7.3 %broadcast_multiply_fusion.5 = f32[64,128,256]{2,1,0:T(8,128)} fusion(f32[64]{0:T(128)S(1)} %fusion.40, bf16[64,128,256]{2,1,0:T(8,128)(2,1)} %gather_fusion.1, bf16[2,64,128,128]{2,3,1,0:T(8,128)(2,1)} %get-tuple-element.259, s32[]{:T(128)} %get-tuple-element.248), kind=kOutput, calls=%fused_computation.19.clone.1 | convolution fusion | flops 538968064 | bytes 14680832 | tf_op jit(solution)/shard_map/while/body/eval_jaxpr/bji,bjf->bif/dot_general | solution.py:59
  154.1 12.4 %scatter_fusion.1 = f32[8,128,256]{2,1,0:T(8,128)S(1)} fusion(f32[8,128,256]{2,1,0:T(8,128)S(1)} %get-tuple-element.249, s32[64]{0:T(128)S(1)} %get-tuple-element.214, f32[64,128,256]{2,1,0:T(8,128)} %broadcast_multiply_fusion.5), kind=kCustom, calls=%fused_computation.3.clone.1 | custom fusion | flops 2097152 | bytes 25166080 | tf_op jit(solution)/shard_map/while/body/eval_jaxpr/scatter-add | solution.py:60
  166.5 4.0 %gather_fusion.1 = bf16[64,128,256]{2,1,0:T(8,128)(2,1)} fusion(bf16[16,128,256]{2,1,0:T(8,128)(2,1)} %get-tuple-element.261, s32[1024]{0:T(1024)S(1)} %pad_clamp_fusion.5), kind=kCustom, calls=%fused_computation.1.clone.1 | custom fusion | bytes 8388864 | tf_op jit(solution)/shard_map/while/body/eval_jaxpr/gather | solution.py:58
  170.6 7.3 %broadcast_multiply_fusion.5 = f32[64,128,256]{2,1,0:T(8,128)} fusion(f32[64]{0:T(128)S(1)} %fusion.40, bf16[64,128,256]{2,1,0:T(8,128)(2,1)} %gather_fusion.1, bf16[2,64,128,128]{2,3,1,0:T(8,128)(2,1)} %get-tuple-element.259, s32[]{:T(128)} %get-tuple-element.248), kind=kOutput, calls=%fused_computation.19.clone.1 | convolution fusion | flops 538968064 | bytes 14680832 | tf_op jit(solution)/shard_map/while/body/eval_jaxpr/bji,bjf->bif/dot_general | solution.py:59
  177.8 12.4 %scatter_fusion.1 = f32[8,128,256]{2,1,0:T(8,128)S(1)} fusion(f32[8,128,256]{2,1,0:T(8,128)S(1)} %get-tuple-element.249, s32[64]{0:T(128)S(1)} %get-tuple-element.214, f32[64,128,256]{2,1,0:T(8,128)} %broadcast_multiply_fusion.5), kind=kCustom, calls=%fused_computation.3.clone.1 | custom fusion | flops 2097152 | bytes 25166080 | tf_op jit(solution)/shard_map/while/body/eval_jaxpr/scatter-add | solution.py:60
  190.3 1.0 copy.14
  191.4 20.2 %psum.7 = f32[32,256]{1,0:T(8,128)S(1)} all-reduce(bf16[32,256]{1,0:T(8,128)(2,1)} %reduce-scatter.8.cloned.1.call-done), channel_id=1, replica_groups=mesh['row'=4,'col'=2,'rep'=4] {'row'}, use_global_device_ids=true, to_apply=%region_9.10 | all-reduce | flops 8192 | bytes 49152 | tf_op jit(solution)/shard_map/psum | solution.py:50
  211.6 9.2 %all_gather.11 = f32[256,256]{1,0:T(8,128)S(1)} all-gather(f32[32,256]{1,0:T(8,128)S(1)} %psum.7), channel_id=1, replica_groups=mesh['row'=4,'col'=2,'rep'=4] {'col','rep'}, dimensions={0}, use_global_device_ids=true | all-gather | bytes 294912 | tf_op jit(solution)/shard_map/all_gather | solution.py:51
  (39 shorter events, 3.4 us)
Async XLA Ops:
  7.2 109.2 %copy-start = (bf16[256,256]{1,0:T(8,128)(2,1)S(1)}, bf16[256,256]{1,0:T(8,128)(2,1)}, u32[]{:S(2)}) copy-start(bf16[256,256]{1,0:T(8,128)(2,1)} %param.11) | copy-start | bytes 393220
  7.2 109.2 %reduce-scatter.4.cloned.1.call-start = ((), (), s32[]{:S(2)}) async-start(), calls=%async_computation.3 | async-start | bytes 2359296 | tf_op jit(solution)/shard_map/reduce_scatter | solution.py:38
  26.8 89.6 %copy-start.3 = (bf16[256,256]{1,0:T(8,128)(2,1)S(1)}, bf16[256,256]{1,0:T(8,128)(2,1)}, u32[]{:S(2)}) copy-start(bf16[256,256]{1,0:T(8,128)(2,1)} %param.12) | copy-start | bytes 393220
  71.9 1.4 copy-start.1
  73.3 69.4 %all-gather.2.cloned.1.call-start = ((), (), s32[]{:S(2)}) async-start(), calls=%async_computation.4 | async-start | bytes 1179648 | tf_op jit(solution)/shard_map/all_gather | solution.py:53
  119.2 6.5 %copy-start.2 = (f32[256,256]{1,0:T(8,128)S(1)}, f32[256,256]{1,0:T(8,128)}, u32[]{:S(2)}) copy-start(f32[256,256]{1,0:T(8,128)} %reduce-scatter.4.cloned.1.call-done) | copy-start | bytes 786436
  119.2 72.1 %reduce-scatter.8.cloned.1.call-start = ((), (), s32[]{:S(2)}) async-start(), calls=%async_computation.6 | async-start | bytes 147456 | tf_op jit(solution)/shard_map/reduce_scatter | solution.py:47
  126.5 94.3 %reduce-scatter.6.cloned.1.call-start = ((), (), s32[]{:S(2)}) async-start(), calls=%async_computation.5 | async-start | bytes 655360 | tf_op jit(solution)/shard_map/reduce_scatter | solution.py:66
Sparse Core Ops, SparseCore 0:
  73.4 42.9 reduce-scatter.3
  119.3 23.3 all-gather.1
  146.3 33.5 reduce-scatter.7
  191.4 22.2 reduce-scatter.5
where the time goes:
time: 229 us; the launch traced here: 228 us
  waiting for transfers between devices  59.2 us (26%)
  other arithmetic  49.7 us (22%)
  blocking collectives  47 us (21%)
  matrix products  32.8 us (14%)
  local copies, waits for them, and re-layouts  24.5 us (11%)
  between operations  14.5 us (6%)
    reduce_scatter x1, waiting for transfers between devices, local(): lax.psum_scatter(partial_value, ('col', 'rep'), scatter_dimension=0, tile...  43 us
    scatter-add x2, other arithmetic, forward_step(): return (total.at[rows_g].add(product * live_g[:, None, None]), None)  24.8 us
    scatter-add x2, other arithmetic, backward_step(): return (total.at[cols_g].add(product * live_g[:, None, None]), None)  24.8 us
    psum x1, blocking collectives, local(): share = lax.psum(share, 'row')  20.2 us
    all_gather x1, blocking collectives, local(): gathered = lax.all_gather(features, 'row', axis=1, tiled=True)  17.6 us
    all_gather x1, waiting for transfers between devices, local(): back_all = lax.all_gather(back_rows, ('col', 'rep'), axis=0, tiled=True)  16.1 us
    dot_general x2, matrix products, forward_step(): jnp.einsum('bij,bjf->bif', blocks_g, chosen, preferred_element_type=jnp.f...  14.6 us
    dot_general x2, matrix products, backward_step(): jnp.einsum('bji,bjf->bif', blocks_g, chosen, preferred_element_type=jnp.f...  14.6 us
  transfers between devices with their start and end apart: 4, of which 2 were waited for; matrix products, arithmetic and copies ran while one was open for 24% of the time, Pallas kernels for 0%

commit v1 on v0

--- a/solution.py
+++ b/solution.py
@@ -50,7 +50,12 @@
     share = lax.psum(share, "row")
     weight_grad = lax.all_gather(share, ("col", "rep"), axis=0, tiled=True)
     back_rows = jnp.dot(grad_pre, weight.T, preferred_element_type=jnp.float32).astype(jnp.bfloat16)
-    back_all = lax.all_gather(back_rows, ("col", "rep"), axis=0, tiled=True)
+    back_all = jnp.concatenate(
+        lax.all_to_all(
+            jnp.stack([back_rows] * lax.axis_size(("col", "rep"))), ("col", "rep"), 0, 0
+        ),
+        axis=0,
+    )
     back_blocks = back_all.reshape(row_blocks, 128, back_all.shape[1])
 
     def backward_step(total, piece):

time: 229 us -> 221 us (0.965)
  waiting for transfers between devices: 59.2 us -> 50.1 us
  starting transfers between devices: 0.16 us -> 3.68 us
    all_gather x1 -> x0, waiting for transfers between devices: 16.1 us -> none  [local(): back_all = lax.all_gather(back_rows, ('col', 'rep'), axis=0, tiled=True)]
    all_to_all x0 -> x1, waiting for transfers between devices: none -> 6.99 us  [local(): lax.all_to_all(jnp.stack([back_rows] * lax.axis_size(('col', 'rep'))), ('...]
    all_to_all x0 -> x1, starting transfers between devices: none -> 3.56 us  [local(): lax.all_to_all(jnp.stack([back_rows] * lax.axis_size(('col', 'rep'))), ('...]
    gather x2, local copies, waits for them, and re-layouts: 8 us -> 5.55 us  [backward_step(): chosen = back_blocks[rows_g]]
where the time goes in v1:
time: 221 us
  waiting for transfers between devices  50.1 us (23%)
  other arithmetic  49.7 us (22%)
  blocking collectives  47.1 us (21%)
  matrix products  32.2 us (15%)
  local copies, waits for them, and re-layouts  23.1 us (10%)
  between operations  14.5 us (7%)
  starting transfers between devices  3.68 us (2%)
    reduce_scatter x1, waiting for transfers between devices, local(): lax.psum_scatter(partial_value, ('col', 'rep'), scatter_dimension=0, tile...  43.1 us
    scatter-add x2, other arithmetic, forward_step(): return (total.at[rows_g].add(product * live_g[:, None, None]), None)  24.8 us
    scatter-add x2, other arithmetic, backward_step(): return (total.at[cols_g].add(product * live_g[:, None, None]), None)  24.7 us
    psum x1, blocking collectives, local(): share = lax.psum(share, 'row')  20.2 us
    all_gather x1, blocking collectives, local(): gathered = lax.all_gather(features, 'row', axis=1, tiled=True)  17.6 us
    dot_general x2, matrix products, backward_step(): jnp.einsum('bji,bjf->bif', blocks_g, chosen, preferred_element_type=jnp.f...  14.6 us
    dot_general x2, matrix products, forward_step(): jnp.einsum('bij,bjf->bif', blocks_g, chosen, preferred_element_type=jnp.f...  14.6 us
    all_gather x1, blocking collectives, local(): weight_grad = lax.all_gather(share, ('col', 'rep'), axis=0, tiled=True)  9.31 us
  transfers between devices with their start and end apart: 4, of which 2 were waited for; matrix products, arithmetic and copies ran while one was open for 24% of the time, Pallas kernels for 0%

profile of v1, /device:TPU:0, one launch (start us, length us, event | category | flops | bytes accessed | tf_op | source)
XLA Modules:
  0.0 220.5 jit_solution(17732652784581409749)
XLA Ops:
  8.8 17.6 %all_gather.6 = bf16[1024,256]{0,1:T(8,128)(2,1)S(1)} all-gather(bf16[1024,64]{0,1:T(8,128)(2,1)} %param.10), channel_id=1, replica_groups=mesh['row'=4,'col'=2,'rep'=4] {'row'}, dimensions={1}, use_global_device_ids=true | all-gather | bytes 655360 | tf_op jit(solution)/shard_map/all_gather | solution.py:13
  26.8 45.1 %while.20 = (s32[]{:T(128)}, f32[16,128,256]{2,1,0:T(8,128)S(1)}, s32[2,64]{1,0:T(2,128)S(1)}, bf16[2,64,128,128]{3,2,1,0:T(8,128)(2,1)}, s32[2,64]{1,0:T(2,128)...) while((s32[]{:T(128)}, f32[16,128,256]{2,1,0:T(8,128)S(1)}, ...), condition=%wide.region_2.3_spmd, body=%wide.region_0.2_spmd.sunk | while | flops 541066624 | bytes 48241756 | solution.py:34
  26.9 2.8 %gather_fusion = bf16[64,128,256]{2,1,0:T(8,128)(2,1)} fusion(bf16[8,128,256]{2,1,0:T(8,128)(2,1)S(1)} %get-tuple-element.237, s32[1024]{0:T(1024)S(1)} %pad_clamp_fusion.4), kind=kCustom, calls=%fused_computation.clone.1 | custom fusion | bytes 8388864 | tf_op jit(solution)/shard_map/while/body/eval_jaxpr/gather | solution.py:30
  29.7 7.3 %broadcast_multiply_fusion.4 = f32[64,128,256]{2,1,0:T(8,128)} fusion(f32[64]{0:T(128)S(1)} %fusion.36, bf16[64,128,256]{2,1,0:T(8,128)(2,1)} %gather_fusion, bf16[2,64,128,128]{3,2,1,0:T(8,128)(2,1)} %get-tuple-element.235, s32[]{:T(128)} %get-tuple-element.224), kind=kOutput, calls=%fused_computation.4.clone.1 | convolution fusion | flops 538968064 | bytes 14680832 | tf_op jit(solution)/shard_map/while/body/eval_jaxpr/bij,bjf->bif/dot_general | solution.py:31
  37.0 12.4 %scatter_fusion = f32[16,128,256]{2,1,0:T(8,128)S(1)} fusion(f32[16,128,256]{2,1,0:T(8,128)S(1)} %get-tuple-element.225, s32[64]{0:T(128)S(1)} %get-tuple-element.205, f32[64,128,256]{2,1,0:T(8,128)} %broadcast_multiply_fusion.4), kind=kCustom, calls=%fused_computation.2.clone.1 | custom fusion | flops 2097152 | bytes 25166080 | tf_op jit(solution)/shard_map/while/body/eval_jaxpr/scatter-add | solution.py:32
  49.4 2.8 %gather_fusion = bf16[64,128,256]{2,1,0:T(8,128)(2,1)} fusion(bf16[8,128,256]{2,1,0:T(8,128)(2,1)S(1)} %get-tuple-element.237, s32[1024]{0:T(1024)S(1)} %pad_clamp_fusion.4), kind=kCustom, calls=%fused_computation.clone.1 | custom fusion | bytes 8388864 | tf_op jit(solution)/shard_map/while/body/eval_jaxpr/gather | solution.py:30
  52.2 7.3 %broadcast_multiply_fusion.4 = f32[64,128,256]{2,1,0:T(8,128)} fusion(f32[64]{0:T(128)S(1)} %fusion.36, bf16[64,128,256]{2,1,0:T(8,128)(2,1)} %gather_fusion, bf16[2,64,128,128]{3,2,1,0:T(8,128)(2,1)} %get-tuple-element.235, s32[]{:T(128)} %get-tuple-element.224), kind=kOutput, calls=%fused_computation.4.clone.1 | convolution fusion | flops 538968064 | bytes 14680832 | tf_op jit(solution)/shard_map/while/body/eval_jaxpr/bij,bjf->bif/dot_general | solution.py:31
  59.5 12.4 %scatter_fusion = f32[16,128,256]{2,1,0:T(8,128)S(1)} fusion(f32[16,128,256]{2,1,0:T(8,128)S(1)} %get-tuple-element.225, s32[64]{0:T(128)S(1)} %get-tuple-element.205, f32[64,128,256]{2,1,0:T(8,128)} %broadcast_multiply_fusion.4), kind=kCustom, calls=%fused_computation.2.clone.1 | custom fusion | flops 2097152 | bytes 25166080 | tf_op jit(solution)/shard_map/while/body/eval_jaxpr/scatter-add | solution.py:32
  72.0 1.3 copy-done.1
  73.3 43.1 %reduce-scatter.4.cloned.1.call-done = f32[256,256]{1,0:T(8,128)} async-done(((f32[2048,256]{1,0:T(8,128)}), f32[256,256]{1,0:T(8,128)}) %reduce-scatter.4.cloned.1.call-update) | async-done | bytes 262160 | tf_op jit(solution)/shard_map/reduce_scatter | solution.py:38
  116.4 1.9 multiply_convert_fusion
  118.5 1.1 stack.2
  119.6 3.6 %all-to-all-start = ((bf16[8,256,256]{2,1,0:T(8,128)(2,1)}), bf16[8,256,256]{2,1,0:T(8,128)(2,1)S(1)}, u32[]{:S(2)}, u32[]{:S(2)}) async-start(bf16[8,256,256]{2,1,0:T(8,128)(2,1)} %stack.2), calls=%async_computation.1 | async-start | bytes 2097152 | tf_op jit(solution)/shard_map/all_to_all | solution.py:54
  123.2 6.4 %copy.9 = bf16[1,1,128,128,128]{3,4,2,1,0:T(8,128)(2,1)} copy(bf16[1,1,128,128,128]{4,3,2,1,0:T(8,128)(2,1)} %bitcast.81) | data formatting | bytes 8388608 | tf_op args[3]
  130.5 7.0 %all-to-all-done = bf16[8,256,256]{2,1,0:T(8,128)(2,1)S(1)} async-done(((bf16[8,256,256]{2,1,0:T(8,128)(2,1)}), bf16[8,256,256]{2,1,0:T(8,128)(2,1)S(1)}, u32[]{:S(2)}, u32[]{:S(2)}) %all-to-all-start) | async-done | bytes 1048608 | tf_op jit(solution)/shard_map/all_to_all | solution.py:54
  137.6 45.0 %while.21 = (s32[]{:T(128)}, f32[8,128,256]{2,1,0:T(8,128)S(1)}, s32[2,64]{1,0:T(2,128)S(1)}, bf16[2,64,128,128]{2,3,1,0:T(8,128)(2,1)}, s32[2,64]{1,0:T(2,128)S...) while((s32[]{:T(128)}, f32[8,128,256]{2,1,0:T(8,128)S(1)}, ...), condition=%wide.region_6.7_spmd, body=%wide.region_4.6_spmd.sunk | while | flops 541066624 | bytes 48241756 | solution.py:67
  137.7 2.8 %gather_fusion.1 = bf16[64,128,256]{2,1,0:T(8,128)(2,1)} fusion(bf16[16,128,256]{2,1,0:T(8,128)(2,1)S(1)} %get-tuple-element.261, s32[1024]{0:T(1024)S(1)} %pad_clamp_fusion.5), kind=kCustom, calls=%fused_computation.1.clone.1 | custom fusion | bytes 8388864 | tf_op jit(solution)/shard_map/while/body/eval_jaxpr/gather | solution.py:63
  140.4 7.3 %broadcast_multiply_fusion.5 = f32[64,128,256]{2,1,0:T(8,128)} fusion(f32[64]{0:T(128)S(1)} %fusion.40, bf16[64,128,256]{2,1,0:T(8,128)(2,1)} %gather_fusion.1, bf16[2,64,128,128]{2,3,1,0:T(8,128)(2,1)} %get-tuple-element.259, s32[]{:T(128)} %get-tuple-element.248), kind=kOutput, calls=%fused_computation.19.clone.1 | convolution fusion | flops 538968064 | bytes 14680832 | tf_op jit(solution)/shard_map/while/body/eval_jaxpr/bji,bjf->bif/dot_general | solution.py:64
  147.8 12.4 %scatter_fusion.1 = f32[8,128,256]{2,1,0:T(8,128)S(1)} fusion(f32[8,128,256]{2,1,0:T(8,128)S(1)} %get-tuple-element.249, s32[64]{0:T(128)S(1)} %get-tuple-element.214, f32[64,128,256]{2,1,0:T(8,128)} %broadcast_multiply_fusion.5), kind=kCustom, calls=%fused_computation.3.clone.1 | custom fusion | flops 2097152 | bytes 25166080 | tf_op jit(solution)/shard_map/while/body/eval_jaxpr/scatter-add | solution.py:65
  160.2 2.8 %gather_fusion.1 = bf16[64,128,256]{2,1,0:T(8,128)(2,1)} fusion(bf16[16,128,256]{2,1,0:T(8,128)(2,1)S(1)} %get-tuple-element.261, s32[1024]{0:T(1024)S(1)} %pad_clamp_fusion.5), kind=kCustom, calls=%fused_computation.1.clone.1 | custom fusion | bytes 8388864 | tf_op jit(solution)/shard_map/while/body/eval_jaxpr/gather | solution.py:63
  163.0 7.3 %broadcast_multiply_fusion.5 = f32[64,128,256]{2,1,0:T(8,128)} fusion(f32[64]{0:T(128)S(1)} %fusion.40, bf16[64,128,256]{2,1,0:T(8,128)(2,1)} %gather_fusion.1, bf16[2,64,128,128]{2,3,1,0:T(8,128)(2,1)} %get-tuple-element.259, s32[]{:T(128)} %get-tuple-element.248), kind=kOutput, calls=%fused_computation.19.clone.1 | convolution fusion | flops 538968064 | bytes 14680832 | tf_op jit(solution)/shard_map/while/body/eval_jaxpr/bji,bjf->bif/dot_general | solution.py:64
  170.3 12.4 %scatter_fusion.1 = f32[8,128,256]{2,1,0:T(8,128)S(1)} fusion(f32[8,128,256]{2,1,0:T(8,128)S(1)} %get-tuple-element.249, s32[64]{0:T(128)S(1)} %get-tuple-element.214, f32[64,128,256]{2,1,0:T(8,128)} %broadcast_multiply_fusion.5), kind=kCustom, calls=%fused_computation.3.clone.1 | custom fusion | flops 2097152 | bytes 25166080 | tf_op jit(solution)/shard_map/while/body/eval_jaxpr/scatter-add | solution.py:65
  183.8 20.2 %psum.7 = f32[32,256]{1,0:T(8,128)S(1)} all-reduce(bf16[32,256]{1,0:T(8,128)(2,1)} %reduce-scatter.8.cloned.1.call-done), channel_id=1, replica_groups=mesh['row'=4,'col'=2,'rep'=4] {'row'}, use_global_device_ids=true, to_apply=%region_9.10 | all-reduce | flops 8192 | bytes 49152 | tf_op jit(solution)/shard_map/psum | solution.py:50
  204.0 9.3 %all_gather.7 = f32[256,256]{1,0:T(8,128)S(1)} all-gather(f32[32,256]{1,0:T(8,128)S(1)} %psum.7), channel_id=1, replica_groups=mesh['row'=4,'col'=2,'rep'=4] {'col','rep'}, dimensions={0}, use_global_device_ids=true | all-gather | bytes 294912 | tf_op jit(solution)/shard_map/all_gather | solution.py:51
  (39 shorter events, 4.6 us)
Async XLA Ops:
  7.2 109.2 %copy-start = (bf16[256,256]{1,0:T(8,128)(2,1)S(1)}, bf16[256,256]{1,0:T(8,128)(2,1)}, u32[]{:S(2)}) copy-start(bf16[256,256]{1,0:T(8,128)(2,1)} %param.11) | copy-start | bytes 393220
  7.2 109.2 %reduce-scatter.4.cloned.1.call-start = ((), (), s32[]{:S(2)}) async-start(), calls=%async_computation.4 | async-start | bytes 2359296 | tf_op jit(solution)/shard_map/reduce_scatter | solution.py:38
  26.8 89.6 %copy-start.3 = (bf16[256,256]{1,0:T(8,128)(2,1)S(1)}, bf16[256,256]{1,0:T(8,128)(2,1)}, u32[]{:S(2)}) copy-start(bf16[256,256]{1,0:T(8,128)(2,1)} %param.12) | copy-start | bytes 393220
  71.9 1.4 copy-start.1
  119.6 18.0 %all-to-all-start = ((bf16[8,256,256]{2,1,0:T(8,128)(2,1)}), bf16[8,256,256]{2,1,0:T(8,128)(2,1)S(1)}, u32[]{:S(2)}, u32[]{:S(2)}) async-start(bf16[8,256,256]{2,1,0:T(8,128)(2,1)} %stack.2), calls=%async_computation.1 | async-start | bytes 2097152 | tf_op jit(solution)/shard_map/all_to_all | solution.py:54
  123.1 6.5 %copy-start.2 = (f32[256,256]{1,0:T(8,128)S(1)}, f32[256,256]{1,0:T(8,128)}, u32[]{:S(2)}) copy-start(f32[256,256]{1,0:T(8,128)} %reduce-scatter.4.cloned.1.call-done) | copy-start | bytes 786436
  123.1 60.6 %reduce-scatter.8.cloned.1.call-start = ((), (), s32[]{:S(2)}) async-start(), calls=%async_computation.6 | async-start | bytes 147456 | tf_op jit(solution)/shard_map/reduce_scatter | solution.py:47
  130.5 82.8 %reduce-scatter.6.cloned.1.call-start = ((), (), s32[]{:S(2)}) async-start(), calls=%async_computation.5 | async-start | bytes 655360 | tf_op jit(solution)/shard_map/reduce_scatter | solution.py:71
Sparse Core Ops, SparseCore 0:
  73.4 42.9 reduce-scatter.3
  130.6 34.9 reduce-scatter.7
  183.9 22.0 reduce-scatter.5
